TPU v7x, 32 devices: a whole 2x2x4 slice. The times are simulated.
32 devices in a mesh: band: 4 (over y, x), sector: 8 (over z, core).
Axes of the slice: x: 2, y: 2, z: 4, core: 2. Of those that a mesh axis runs over, the one named last changes fastest.
Arguments:
- grid_lat: bfloat16 [32, 512, 512], P('band', 'sector'), may hold values from -6 to 6
- mesh_lat: bfloat16 [4096, 512], P(('band', 'sector')), may hold values from -6 to 6
- edge_feat: bfloat16 [49152, 512], P(('band', 'sector')), may hold values from -6 to 6
- edge_src: int32 [49152], P(('band', 'sector')), may hold values from 0 to 255, as said below
- edge_dst: int32 [49152], P(('band', 'sector')), may hold values from 0 to 511, as said below
- send_rows: int32 [4096], P(('band', 'sector')), may hold values from 0 to 127
- w_edge1: bfloat16 [1536, 512], replicated, may hold values from -0.15625 to 0.15625
- w_edge2: bfloat16 [512, 512], replicated, may hold values from -0.25 to 0.25
- edge_gain: float32 [512], replicated, may hold values from 0.25 to 1.75
- w_node1: bfloat16 [1024, 512], replicated, may hold values from -0.1875 to 0.1875
- w_node2: bfloat16 [512, 512], replicated, may hold values from -0.25 to 0.25
- node_gain: float32 [512], replicated, may hold values from 0.25 to 1.75
- cotangent: bfloat16 [32, 512, 512], P('band', 'sector'), may hold values from -6 to 6
Outputs:
- grid_out: bfloat16 [32, 512, 512], P('band', 'sector')
- grad_grid: bfloat16 [32, 512, 512], P('band', 'sector')
- grad_mesh: bfloat16 [4096, 512], P(('band', 'sector'))
- grad_w_edge1: float32 [1536, 512], P('sector')
Inputs may be any that keep to these rules, and one draw needn't show every extreme that they name: `edge_src`: A device's mesh table is its 128 own rows followed by 32 rows each from the sector neighbour below, the sector neighbour above, the band neighbour below and the band neighbour above; devices of the first band never read the rows from below, those of the last band never the rows from above. `edge_dst`: each grid point of a device is the destination of exactly 3 of that device's edges; edges are in no particular order.
All inputs are finite; a program needn't handle non-finite values.
Results may differ from a plain program's by a relative error of at most 0.02.
Values may be sent and summed in bfloat16 or wider, within the bound.
A program may use at most 64 MiB of HBM per device.

v0:
```python
import math
import jax
import jax.numpy as jnp
from jax import lax
from jax.sharding import PartitionSpec as P

EPSILON = 1e-05


def with_halo(shard, sides, width, wrap):
    for axis, dim in sides:
        devices, length = (lax.axis_size(axis), shard.shape[dim])
        up = [(i, (i + 1) % devices) for i in range(devices if wrap else devices - 1)]
        down = [(j, i) for i, j in up]
        last = lax.slice_in_dim(shard, length - width, length, axis=dim)
        initial = lax.slice_in_dim(shard, 0, width, axis=dim)
        before = lax.ppermute(last, axis, up)
        after = lax.ppermute(initial, axis, down)
        shard = jnp.concatenate([before, shard, after], axis=dim)
    return shard


def swish(values):
    return values * jax.nn.sigmoid(values)


def layer_norm(values, gain_vector):
    average = jnp.mean(values, axis=-1, keepdims=True)
    centred = values - average
    spread = jnp.mean(centred * centred, axis=-1, keepdims=True)
    return centred * lax.rsqrt(spread + EPSILON) * gain_vector


def decode_tail(pre_act, grid_wide, edge_dst, w_edge2, edge_gain, w_node1, w_node2, node_gain):
    hidden = swish(pre_act).astype(jnp.bfloat16)
    edge_raw = jnp.dot(hidden, w_edge2, preferred_element_type=jnp.float32)
    message = layer_norm(edge_raw, edge_gain).astype(jnp.bfloat16)
    points = grid_wide.shape[0]
    onehot = (edge_dst[None, :] == jnp.arange(points, dtype=jnp.int32)[:, None]).astype(
        jnp.bfloat16
    )
    aggregated = jnp.dot(onehot, message, preferred_element_type=jnp.float32).astype(jnp.bfloat16)
    node_input = jnp.concatenate([aggregated, grid_wide.astype(jnp.bfloat16)], axis=1)
    node_hidden = swish(jnp.dot(node_input, w_node1, preferred_element_type=jnp.float32)).astype(
        jnp.bfloat16
    )
    node_raw = jnp.dot(node_hidden, w_node2, preferred_element_type=jnp.float32)
    return (grid_wide + layer_norm(node_raw, node_gain)).astype(jnp.bfloat16)


def shards(
    grid_lat,
    mesh_lat,
    edge_feat,
    edge_src,
    edge_dst,
    send_rows,
    w_edge1,
    w_edge2,
    edge_gain,
    w_node1,
    w_node2,
    node_gain,
    cotangent,
):
    feature_width = w_edge2.shape[0]
    lat_rows = grid_lat.shape[0]
    lon_cols = grid_lat.shape[1]
    grid_block = grid_lat.reshape(lat_rows * lon_cols, feature_width)
    cot_block = cotangent.reshape(lat_rows * lon_cols, feature_width)
    own_rows = mesh_lat.shape[0]
    margin = send_rows.shape[0] // 4
    picked = jnp.take(mesh_lat, send_rows, axis=0)
    sector_recv = with_halo(picked[: 2 * margin], (("sector", 0),), margin, True)
    band_recv = with_halo(picked[2 * margin :], (("band", 0),), margin, False)
    mesh_table = jnp.concatenate(
        [
            mesh_lat,
            sector_recv[:margin],
            sector_recv[3 * margin :],
            band_recv[:margin],
            band_recv[3 * margin :],
        ],
        axis=0,
    )
    inputs = jnp.concatenate([edge_feat, mesh_table[edge_src], grid_block[edge_dst]], axis=1)
    pre_act = jnp.dot(inputs, w_edge1, preferred_element_type=jnp.float32)
    grid_wide = grid_block.astype(jnp.float32)

    def finish(pre_values, grid_values):
        return decode_tail(
            pre_values, grid_values, edge_dst, w_edge2, edge_gain, w_node1, w_node2, node_gain
        )

    result, pullback = jax.vjp(finish, pre_act, grid_wide)
    grad_pre, grad_tail = pullback(cot_block)
    grad_pre_b = grad_pre.astype(jnp.bfloat16)
    grad_inputs = lax.dot_general(
        grad_pre_b,
        w_edge1[feature_width:],
        (((1,), (1,)), ((), ())),
        preferred_element_type=jnp.float32,
    )
    grad_table = jax.ops.segment_sum(
        grad_inputs[:, :feature_width], edge_src, num_segments=mesh_table.shape[0]
    )
    grad_grid = grad_tail + jax.ops.segment_sum(
        grad_inputs[:, feature_width:], edge_dst, num_segments=grid_block.shape[0]
    )
    sector_back = with_halo(
        grad_table[own_rows : own_rows + 2 * margin].astype(jnp.bfloat16),
        (("sector", 0),),
        margin,
        True,
    ).astype(jnp.float32)
    band_back = with_halo(
        grad_table[own_rows + 2 * margin :].astype(jnp.bfloat16), (("band", 0),), margin, False
    ).astype(jnp.float32)
    returned = jnp.concatenate(
        [
            sector_back[:margin],
            sector_back[3 * margin :],
            band_back[:margin],
            band_back[3 * margin :],
        ],
        axis=0,
    )
    grad_mesh = (
        grad_table[:own_rows] + jax.ops.segment_sum(returned, send_rows, num_segments=own_rows)
    ).astype(jnp.bfloat16)
    total_edges = edge_feat.shape[0] * lax.axis_size("band") * lax.axis_size("sector")
    grad_scale = 1.0 / math.sqrt(total_edges)
    sector_part = lax.psum_scatter(
        lax.dot_general(
            inputs, grad_pre_b, (((0,), (0,)), ((), ())), preferred_element_type=jnp.float32
        ).astype(jnp.bfloat16),
        "sector",
        scatter_dimension=0,
        tiled=True,
    )
    share_rows = lax.psum(sector_part, "band").astype(jnp.float32)
    grad_w_edge1 = share_rows * grad_scale
    grid_out = result.reshape(lat_rows, lon_cols, feature_width)
    grad_grid_out = grad_grid.astype(jnp.bfloat16).reshape(lat_rows, lon_cols, feature_width)
    return (grid_out, grad_grid_out, grad_mesh, grad_w_edge1)


def solution(mesh):
    in_specs = (
        P("band", "sector", None),
        P(("band", "sector"), None),
        P(("band", "sector"), None),
        P(("band", "sector")),
        P(("band", "sector")),
        P(("band", "sector")),
        P(),
        P(),
        P(),
        P(),
        P(),
        P(),
        P("band", "sector", None),
    )
    out_specs = (
        P("band", "sector", None),
        P("band", "sector", None),
        P(("band", "sector"), None),
        P("sector", None),
    )
    return jax.shard_map(shards, mesh=mesh, in_specs=in_specs, out_specs=out_specs, check_vma=False)
```

profile of v0, /device:TPU:0, one launch (start us, length us, event | category | flops | bytes accessed | tf_op | source)
XLA Modules:
  0.0 159.2 jit_solution(11389695265624207588)
XLA Ops:
  7.2 0.8 compare_and_fusion
  8.0 0.7 compare_select_fusion.2
  8.7 1.8 %gather_fusion = bf16[128,512]{1,0:T(8,128)(2,1)S(1)} fusion(bf16[128,512]{1,0:T(8,128)(2,1)} %param.14, s32[1024]{0:T(1024)S(1)} %pad_clamp_fusion.2), kind=kCustom, calls=%fused_computation | custom fusion | bytes 262656 | tf_op jit(solution)/shard_map/jit(_take)/gather | solution.py:73
  10.6 0.7 fusion.66
  11.2 1.3 collective-permute-start.3
  12.5 5.5 %collective-permute-start.2 = (bf16[32,512]{1,0:T(8,128)(2,1)}, bf16[32,512]{1,0:T(8,128)(2,1)S(1)}, u32[]{:S(2)}, u32[]{:S(2)}) collective-permute-start(bf16[32,512]{1,0:T(8,128)(2,1)} %get-tuple-element.20), channel_id=1, source_target_pairs={{0,8},{8,16},{16,24},{1,9},{9,17},{17,25},{2,10},{10,18},{18,26},{... | collective-permute-start | bytes 98312 | tf_op jit(solution)/shard_map/ppermute | solution.py:17
  18.0 3.1 %collective-permute-start.1 = (bf16[32,512]{1,0:T(8,128)(2,1)}, bf16[32,512]{1,0:T(8,128)(2,1)S(1)}, u32[]{:S(2)}, u32[]{:S(2)}) collective-permute-start(bf16[32,512]{1,0:T(8,128)(2,1)} %get-tuple-element.21), channel_id=1, source_target_pairs={{1,0},{2,1},{3,2},{4,3},{5,4},{6,5},{7,6},{0,7},{9,8},{10,9},{11,1... | collective-permute-start | bytes 98312 | tf_op jit(solution)/shard_map/ppermute | solution.py:18
  21.1 0.9 constant_dynamic-update-slice_fusion.4
  22.0 0.7 compare_select_fusion.1
  22.7 0.7 compare_select_fusion
  23.4 2.7 %constant_dynamic-update-slice_fusion.7 = bf16[1536,1536]{1,0:T(8,128)(2,1)} fusion(bf16[1536,512]{1,0:T(8,128)(2,1)} %param.15), kind=kLoop, calls=%fused_computation.96 | loop fusion | bytes 3145728
  26.1 4.8 %gather_fusion.2 = bf16[1536,512]{1,0:T(8,128)(2,1)S(1)} fusion(bf16[512,512]{1,0:T(8,128)(2,1)S(1)} %bitcast.21, s32[2048]{0:T(1024)S(1)} %pad_clamp_fusion), kind=kCustom, calls=%fused_computation.2 | custom fusion | bytes 3151872 | tf_op jit(solution)/shard_map/gather | solution.py:86
  31.0 5.4 %gather_fusion.1 = bf16[1536,512]{1,0:T(8,128)(2,1)} fusion(bf16[256,512]{1,0:T(8,128)(2,1)S(1)} %constant_dynamic-update-slice_fusion, s32[2048]{0:T(1024)S(1)} %pad_clamp_fusion.1), kind=kCustom, calls=%fused_computation.1 | custom fusion | bytes 3151872 | tf_op jit(solution)/shard_map/gather | solution.py:86
  36.5 2.8 %constant_dynamic-update-slice_fusion.6 = bf16[1536,1536]{1,0:T(8,128)(2,1)} fusion(bf16[1536,1536]{1,0:T(8,128)(2,1)} %constant_dynamic-update-slice_fusion.7, bf16[1536,512]{1,0:T(8,128)(2,1)} %gather_fusion.1), kind=kLoop, calls=%fused_computation.95 | loop fusion | bytes 3145728
  39.3 1.3 constant_dynamic-update-slice_fusion.5
  40.6 4.5 %fusion.69 = f32[1536,512]{1,0:T(8,128)S(1)} fusion(bf16[1536,1536]{1,0:T(8,128)(2,1)} %constant_dynamic-update-slice_fusion.5, bf16[1536,512]{1,0:T(8,128)(2,1)S(1)} %copy-done.8), kind=kOutput, calls=%fused_computation.122 | convolution fusion | flops 2415919104 | bytes 9437184 | tf_op jit(solution)/shard_map/dot_general | solution.py:87
  45.1 1.2 fusion.67
  46.3 0.5 copy-done.14
  46.8 0.4 multiply_reduce_fusion.1
  47.2 0.3 copy-done.6
  47.5 1.2 fusion.24
  48.7 0.7 fusion.32
  49.4 0.3 copy-done.9
  49.7 0.5 fusion.68
  50.3 0.5 copy-done.13
  50.7 0.4 copy-done.4
  51.1 0.4 fusion.27
  51.6 1.3 fusion.63
  52.9 3.6 %convolution_convert_fusion.1 = bf16[512,1024]{1,0:T(8,128)(2,1)} fusion(bf16[1024,512]{1,0:T(8,128)(2,1)S(1)} %copy-done, f32[512,512]{1,0:T(8,128)} %copy-done.13, bf16[512,512]{1,0:T(8,128)(2,1)} %param.23, f32[512,512]{1,0:T(8,128)S(1)} %get-tuple-element.7, f32[512]{0:T(512)S(1)} %negate_multiply_fusion.1), kind=kOutput, calls=%fused_computation.40 | convolution fusion | flops 808976384 | bytes 4720640 | tf_op jit(solution)/shard_map/transpose(jvp())/dot_general | solution.py:44
  56.5 3.5 %multiply_reduce_fusion = (f32[1536]{0:T(1024)S(1)}, bf16[1536,512]{0,1:T(8,128)(2,1)S(1)}) fusion(f32[1536,512]{0,1:T(8,128)} %copy-done.2, f32[512]{0:T(512)S(1)} %copy-done.7, f32[1536]{0:T(1024)S(1)} %broadcast_multiply_fusion, bf16[512,1024]{1,0:T(8,128)(2,1)} %convolution_convert_fusion.1, s32[1536]{0:T(1024)S(1)} %copy-done.6), kind=kOutput, calls=%fused_computation.19 | convolution fusion | flops 810809856 | bytes 5263360 | tf_op jit(solution)/shard_map/transpose(jvp())/dot_general | solution.py:42
  60.0 0.9 fusion.45
  61.0 1.0 copy-done.15
  62.0 2.4 %fusion.1 = bf16[1536,512]{1,0:T(8,128)(2,1)S(1)} fusion(f32[1536,512]{1,0:T(8,128)S(1)} %copy-done.15, bf16[512,512]{1,0:T(8,128)(2,1)S(1)} %copy-done.11, f32[1536]{0:T(1024)S(1)} %negate_multiply_fusion, bf16[1536,512]{0,1:T(8,128)(2,1)S(1)} %get-tuple-element.30, f32[1536,512]{0,1:T(8,128)S(1)} %copy-done.3, f32[1536]{0:T(1024)S(1)} %multiply_multiply_fusion, ...), kind=kOutput, calls=%fused_computation.11 | convolution fusion | flops 821035008 | bytes 9988096 | tf_op jit(solution)/shard_map/transpose(jvp())/dot_general | solution.py:36
  64.5 1.2 copy-done.12
  65.7 3.8 %convolution_convert_fusion = bf16[1536,512]{1,0:T(8,128)(2,1)} fusion(bf16[1536,1536]{1,0:T(8,128)(2,1)S(1)} %bitcast.26, bf16[1536,512]{1,0:T(8,128)(2,1)S(1)} %fusion.1), kind=kOutput, calls=%fused_computation.30 | convolution fusion | flops 2416705536 | bytes 7864320 | tf_op jit(solution)/shard_map/dot_general | solution.py:134
  69.5 6.2 %fusion.36 = f32[1536,1024]{1,0:T(8,128)} fusion(bf16[1536,512]{1,0:T(8,128)(2,1)} %copy-done.12, bf16[1536,512]{1,0:T(8,128)(2,1)} %param.19), kind=kOutput, calls=%fused_computation.56 | convolution fusion | flops 1610612736 | bytes 8912896 | tf_op jit(solution)/shard_map/dot_general | solution.py:98
  75.7 10.7 %scatter_custom_fusion.1 = f32[256,512]{1,0:T(8,128)S(1)} fusion(s32[1536]{0:T(1024)} %param.16, f32[1536,1024]{1,0:T(8,128)} %fusion.36, f32[]{:T(128)} %constant.21.clone.1), kind=kCustom, calls=%fused_computation.13 | custom fusion | flops 786432 | bytes 3670528 | tf_op jit(solution)/shard_map/scatter-add | solution.py:104
  86.5 1.3 collective-permute-start.7
  87.8 4.9 %collective-permute-start.6 = (bf16[32,512]{1,0:T(8,128)(2,1)S(1)}, bf16[32,512]{1,0:T(8,128)(2,1)S(1)}, u32[]{:S(2)}, u32[]{:S(2)}) collective-permute-start(bf16[32,512]{1,0:T(8,128)(2,1)S(1)} %get-tuple-element.11), channel_id=1, source_target_pairs={{0,8},{8,16},{16,24},{1,9},{9,17},{17,25},{2,10},{10,18},{18,26},{... | collective-permute-start | bytes 98312 | tf_op jit(solution)/shard_map/ppermute | solution.py:17
  92.6 1.2 convert_add_fusion
  93.9 10.9 %scatter_custom_fusion = f32[512,512]{1,0:T(8,128)S(1)} fusion(f32[512,512]{1,0:T(8,128)S(1)} %convert_add_fusion, s32[1536]{0:T(1024)S(1)} %copy-done.6, f32[1536,1024]{1,0:T(8,128)} %fusion.36), kind=kCustom, calls=%fused_computation.15 | custom fusion | flops 786432 | bytes 4194304 | tf_op jit(solution)/shard_map/scatter-add | solution.py:107
  104.7 0.9 convert_element_type.91
  105.6 3.5 %collective-permute-start.5 = (bf16[32,512]{1,0:T(8,128)(2,1)S(1)}, bf16[32,512]{1,0:T(8,128)(2,1)S(1)}, u32[]{:S(2)}, u32[]{:S(2)}) collective-permute-start(bf16[32,512]{1,0:T(8,128)(2,1)S(1)} %get-tuple-element.12), channel_id=1, source_target_pairs={{1,0},{2,1},{3,2},{4,3},{5,4},{6,5},{7,6},{0,7},{9,8},{10,9},{11,1... | collective-permute-start | bytes 98312 | tf_op jit(solution)/shard_map/ppermute | solution.py:18
  109.2 1.5 collective-permute-done.4
  110.8 1.6 %scatter_custom_fusion.2 = f32[128,512]{1,0:T(8,128)S(1)} fusion(f32[128,512]{1,0:T(8,128)S(1)} %slice.96, s32[128]{0:T(128)} %param.18, f32[32,512]{1,0:T(8,128)S(1)} %get-tuple-element.18, f32[]{:T(128)} %constant.48, f32[32,512]{1,0:T(8,128)S(1)} %get-tuple-element.17, f32[32,512]{1,0:T(8,128)S(1)} %get-tuple-element.16, f32[32,512]{1,0:T(8,128)S(1)} %get-tuple-element.15), kind=kCustom, calls=%fused_computation.69 | custom fusion | flops 262144 | bytes 524800 | tf_op jit(solution)/shard_map/scatter-add | solution.py:129
  112.4 0.7 convert_element_type.94
  113.1 37.6 %all-reduce.2.cloned.1.call-done = bf16[192,512]{1,0:T(8,128)(2,1)} async-done(((bf16[192,512]{1,0:T(8,128)(2,1)}), bf16[192,512]{1,0:T(8,128)(2,1)}) %all-reduce.2.cloned.1.call-update) | async-done | bytes 196624 | tf_op jit(solution)/shard_map/psum | solution.py:141
  150.6 1.7 %convert_multiply_fusion.6 = f32[192,512]{1,0:T(8,128)} fusion(bf16[192,512]{1,0:T(8,128)(2,1)} %all-reduce.2.cloned.1.call-done), kind=kLoop, calls=%fused_computation.68 | loop fusion | flops 196608 | bytes 589824 | tf_op jit(solution)/shard_map/mul | solution.py:142
  (65 shorter events, 0.6 us)
Async XLA Ops:
  7.2 41.5 %copy-start = (bf16[1024,512]{1,0:T(8,128)(2,1)S(1)}, bf16[1024,512]{1,0:T(8,128)(2,1)}, u32[]{:S(2)}) copy-start(bf16[1024,512]{1,0:T(8,128)(2,1)} %param.22) | copy-start | bytes 3145732
  7.2 19.0 %copy-start.1 = (bf16[8,64,512]{2,1,0:T(8,128)(2,1)S(1)}, bf16[8,64,512]{2,1,0:T(8,128)(2,1)}, u32[]{:S(2)}) copy-start(bf16[8,64,512]{2,1,0:T(8,128)(2,1)} %param.13) | copy-start | bytes 1572868
  7.2 102.0 %reduce-scatter.2.cloned.1.call-start = ((), (), s32[]{:S(2)}) async-start(), calls=%async_computation.1 | async-start | bytes 1769472 | tf_op jit(solution)/shard_map/reduce_scatter | solution.py:133
  11.2 19.8 %collective-permute-start.3 = (bf16[32,512]{1,0:T(8,128)(2,1)}, bf16[32,512]{1,0:T(8,128)(2,1)S(1)}, u32[]{:S(2)}, u32[]{:S(2)}) collective-permute-start(bf16[32,512]{1,0:T(8,128)(2,1)} %get-tuple-element.19), channel_id=1, source_target_pairs={{8,0},{16,8},{24,16},{9,1},{17,9},{25,17},{10,2},{18,10},{26,18},{... | collective-permute-start | bytes 98312 | tf_op jit(solution)/shard_map/ppermute | solution.py:18
  12.5 18.5 %collective-permute-start.2 = (bf16[32,512]{1,0:T(8,128)(2,1)}, bf16[32,512]{1,0:T(8,128)(2,1)S(1)}, u32[]{:S(2)}, u32[]{:S(2)}) collective-permute-start(bf16[32,512]{1,0:T(8,128)(2,1)} %get-tuple-element.20), channel_id=1, source_target_pairs={{0,8},{8,16},{16,24},{1,9},{9,17},{17,25},{2,10},{10,18},{18,26},{... | collective-permute-start | bytes 98312 | tf_op jit(solution)/shard_map/ppermute | solution.py:17
  18.0 13.0 %collective-permute-start.1 = (bf16[32,512]{1,0:T(8,128)(2,1)}, bf16[32,512]{1,0:T(8,128)(2,1)S(1)}, u32[]{:S(2)}, u32[]{:S(2)}) collective-permute-start(bf16[32,512]{1,0:T(8,128)(2,1)} %get-tuple-element.21), channel_id=1, source_target_pairs={{1,0},{2,1},{3,2},{4,3},{5,4},{6,5},{7,6},{0,7},{9,8},{10,9},{11,1... | collective-permute-start | bytes 98312 | tf_op jit(solution)/shard_map/ppermute | solution.py:18
  21.1 9.9 %collective-permute-start = (bf16[32,512]{1,0:T(8,128)(2,1)}, bf16[32,512]{1,0:T(8,128)(2,1)S(1)}, u32[]{:S(2)}, u32[]{:S(2)}) collective-permute-start(bf16[32,512]{1,0:T(8,128)(2,1)} %get-tuple-element.22), channel_id=1, source_target_pairs={{0,1},{1,2},{2,3},{3,4},{4,5},{5,6},{6,7},{7,0},{8,9},{9,10},{10,1... | collective-permute-start | bytes 98312 | tf_op jit(solution)/shard_map/ppermute | solution.py:17
  36.5 4.1 %copy-start.8 = (bf16[1536,512]{1,0:T(8,128)(2,1)S(1)}, bf16[1536,512]{1,0:T(8,128)(2,1)}, u32[]{:S(2)}) copy-start(bf16[1536,512]{1,0:T(8,128)(2,1)} %param.19) | copy-start | bytes 4718596
  40.6 4.5 %copy-start.10 = (bf16[512,512]{1,0:T(8,128)(2,1)S(1)}, bf16[512,512]{1,0:T(8,128)(2,1)}, u32[]{:S(2)}) copy-start(bf16[512,512]{1,0:T(8,128)(2,1)} %param.20) | copy-start | bytes 1572868
  45.1 1.6 %copy-start.14 = (f32[1536,512]{1,0:T(8,128)}, f32[1536,512]{1,0:T(8,128)S(1)}, u32[]{:S(2)}) copy-start(f32[1536,512]{1,0:T(8,128)S(1)} %fusion.69) | copy-start | bytes 9437188
  46.8 1.9 %copy-start.2 = (f32[1536,512]{0,1:T(8,128)}, f32[1536,512]{0,1:T(8,128)S(1)}, u32[]{:S(2)}) copy-start(f32[1536,512]{0,1:T(8,128)S(1)} %get-tuple-element.26) | copy-start | bytes 9437188
  46.8 0.7 copy-start.6
  46.8 0.7 copy-start.7
  48.7 1.0 copy-start.9
  49.7 1.0 copy-start.13
  49.7 1.4 copy-start.4
  49.7 1.4 copy-start.5
  56.5 3.5 %copy-start.3 = (f32[1536,512]{0,1:T(8,128)S(1)}, f32[1536,512]{0,1:T(8,128)}, u32[]{:S(2)}) copy-start(f32[1536,512]{0,1:T(8,128)} %copy-done.2) | copy-start | bytes 9437188
  60.0 1.0 copy-start.11
  60.0 2.1 %copy-start.15 = (f32[1536,512]{1,0:T(8,128)S(1)}, f32[1536,512]{1,0:T(8,128)}, u32[]{:S(2)}) copy-start(f32[1536,512]{1,0:T(8,128)} %copy-done.14) | copy-start | bytes 9437188
  60.0 5.7 %slice-start = ((s8[4718592]{0:T(1024)(128)(4,1)}), s8[4194304]{0:T(1024)(128)(4,1)S(1)}, s32[]{:S(2)}) async-start(s8[4718592]{0:T(1024)(128)(4,1)} %bitcast.25), calls=%async_computation.3 | async-start | bytes 8388608
  62.0 3.7 %slice-start.1 = ((s8[4718592]{0:T(1024)(128)(4,1)}), s8[524288]{0:T(1024)(128)(4,1)S(1)}, s32[]{:S(2)}) async-start(s8[4718592]{0:T(1024)(128)(4,1)} %bitcast.25), calls=%async_computation.4 | async-start | bytes 1048576
  64.5 1.2 copy-start.12
  69.5 81.1 %all-reduce.2.cloned.1.call-start = ((), (), s32[]{:S(2)}) async-start(), calls=%async_computation.2 | async-start | bytes 393216 | tf_op jit(solution)/shard_map/psum | solution.py:141
  86.5 22.7 %collective-permute-start.7 = (bf16[32,512]{1,0:T(8,128)(2,1)S(1)}, bf16[32,512]{1,0:T(8,128)(2,1)S(1)}, u32[]{:S(2)}, u32[]{:S(2)}) collective-permute-start(bf16[32,512]{1,0:T(8,128)(2,1)S(1)} %get-tuple-element.10), channel_id=1, source_target_pairs={{8,0},{16,8},{24,16},{9,1},{17,9},{25,17},{10,2},{18,10},{26,18},{... | collective-permute-start | bytes 98312 | tf_op jit(solution)/shard_map/ppermute | solution.py:18
  87.8 21.4 %collective-permute-start.6 = (bf16[32,512]{1,0:T(8,128)(2,1)S(1)}, bf16[32,512]{1,0:T(8,128)(2,1)S(1)}, u32[]{:S(2)}, u32[]{:S(2)}) collective-permute-start(bf16[32,512]{1,0:T(8,128)(2,1)S(1)} %get-tuple-element.11), channel_id=1, source_target_pairs={{0,8},{8,16},{16,24},{1,9},{9,17},{17,25},{2,10},{10,18},{18,26},{... | collective-permute-start | bytes 98312 | tf_op jit(solution)/shard_map/ppermute | solution.py:17
  105.6 5.1 %collective-permute-start.4 = (bf16[32,512]{1,0:T(8,128)(2,1)S(1)}, bf16[32,512]{1,0:T(8,128)(2,1)S(1)}, u32[]{:S(2)}, u32[]{:S(2)}) collective-permute-start(bf16[32,512]{1,0:T(8,128)(2,1)S(1)} %get-tuple-element.9), channel_id=1, source_target_pairs={{0,1},{1,2},{2,3},{3,4},{4,5},{5,6},{6,7},{7,0},{8,9},{9,10},{10,1... | collective-permute-start | bytes 98312 | tf_op jit(solution)/shard_map/ppermute | solution.py:17
  105.6 5.1 %collective-permute-start.5 = (bf16[32,512]{1,0:T(8,128)(2,1)S(1)}, bf16[32,512]{1,0:T(8,128)(2,1)S(1)}, u32[]{:S(2)}, u32[]{:S(2)}) collective-permute-start(bf16[32,512]{1,0:T(8,128)(2,1)S(1)} %get-tuple-element.12), channel_id=1, source_target_pairs={{1,0},{2,1},{3,2},{4,3},{5,4},{6,5},{7,6},{0,7},{9,8},{10,9},{11,1... | collective-permute-start | bytes 98312 | tf_op jit(solution)/shard_map/ppermute | solution.py:18
Sparse Core Ops, SparseCore 0:
  69.6 35.2 reduce-scatter.1
  109.3 41.2 all-reduce.1
where the time goes:
time: 160 us; the launch traced here: 159 us
  waiting for transfers between devices  39.1 us (24%)
  other arithmetic  33.7 us (21%)
  matrix products  27.5 us (17%)
  local copies, waits for them, and re-layouts  24.8 us (16%)
  starting transfers between devices  19.6 us (12%)
  between operations  14.4 us (9%)
    psum x1, waiting for transfers between devices, shards(): share_rows = lax.psum(sector_part, 'band').astype(jnp.float32)  37.6 us
    scatter-add x1, other arithmetic, shards(): jax.ops.segment_sum(grad_inputs[:, feature_width:], edge_dst, num_segment...  10.9 us
    unnamed x42, local copies, waits for them, and re-layouts  10.8 us
    scatter-add x1, other arithmetic, shards(): jax.ops.segment_sum(grad_inputs[:, :feature_width], edge_src, num_segment...  10.7 us
    ppermute x4, starting transfers between devices, with_halo(): before = lax.ppermute(last, axis, up)  10.4 us
    ppermute x4, starting transfers between devices, with_halo(): after = lax.ppermute(initial, axis, down)  9.17 us
    dot_general x1, matrix products, shards(): lax.dot_general(grad_pre_b, w_edge1[feature_width:], (((1,), (1,)), ((),...  6.19 us
    gather x1, local copies, waits for them, and re-layouts, shards(): mesh_table[edge_src]  5.42 us
  transfers between devices with their start and end apart: 10, of which 2 were waited for; matrix products, arithmetic and copies ran while one was open for 26% of the time, Pallas kernels for 0%

commit v1 on v0

--- a/solution.py
+++ b/solution.py
@@ -138,7 +138,7 @@
         scatter_dimension=0,
         tiled=True,
     )
-    share_rows = lax.psum(sector_part, "band").astype(jnp.float32)
+    share_rows = jnp.sum(lax.all_gather(sector_part, "band"), axis=0).astype(jnp.float32)
     grad_w_edge1 = share_rows * grad_scale
     grid_out = result.reshape(lat_rows, lon_cols, feature_width)
     grad_grid_out = grad_grid.astype(jnp.bfloat16).reshape(lat_rows, lon_cols, feature_width)

time: 160 us -> 135 us (0.84)
  waiting for transfers between devices: 39.1 us -> 1.61 us
  blocking collectives: 0 us -> 13.8 us
    psum x1 -> x0, waiting for transfers between devices: 37.6 us -> none  [shards(): share_rows = lax.psum(sector_part, 'band').astype(jnp.float32)]
    all_gather x0 -> x1, blocking collectives: none -> 13.8 us  [shards(): lax.all_gather(sector_part, 'band')]
  transfers between devices with their start and end apart: 10 -> 9, of which waited for: 2 -> 1; matrix products, arithmetic and copies ran while one was open for 26% -> 31% of each run, Pallas kernels for 0% -> 0%
where the time goes in v1:
time: 135 us
  other arithmetic  32.9 us (24%)
  matrix products  27.4 us (20%)
  local copies, waits for them, and re-layouts  24.8 us (18%)
  starting transfers between devices  19.6 us (15%)
  between operations  14.4 us (11%)
  blocking collectives  13.8 us (10%)
  waiting for transfers between devices  1.61 us (1%)
    all_gather x1, blocking collectives, shards(): lax.all_gather(sector_part, 'band')  13.8 us
    scatter-add x1, other arithmetic, shards(): jax.ops.segment_sum(grad_inputs[:, feature_width:], edge_dst, num_segment...  10.9 us
    unnamed x42, local copies, waits for them, and re-layouts  10.8 us
    scatter-add x1, other arithmetic, shards(): jax.ops.segment_sum(grad_inputs[:, :feature_width], edge_src, num_segment...  10.6 us
    ppermute x4, starting transfers between devices, with_halo(): before = lax.ppermute(last, axis, up)  10.4 us
    ppermute x4, starting transfers between devices, with_halo(): after = lax.ppermute(initial, axis, down)  9.17 us
    dot_general x1, matrix products, shards(): lax.dot_general(grad_pre_b, w_edge1[feature_width:], (((1,), (1,)), ((),...  6.17 us
    gather x1, local copies, waits for them, and re-layouts, shards(): mesh_table[edge_src]  5.42 us
  transfers between devices with their start and end apart: 9, of which 1 were waited for; matrix products, arithmetic and copies ran while one was open for 31% of the time, Pallas kernels for 0%

profile of v1, /device:TPU:0, one launch (start us, length us, event | category | flops | bytes accessed | tf_op | source)
XLA Modules:
  0.0 134.5 jit_solution(8833025060417392669)
XLA Ops:
  7.2 0.8 compare_and_fusion
  8.0 0.7 compare_select_fusion.2
  8.7 1.8 %gather_fusion = bf16[128,512]{1,0:T(8,128)(2,1)S(1)} fusion(bf16[128,512]{1,0:T(8,128)(2,1)} %param.14, s32[1024]{0:T(1024)S(1)} %pad_clamp_fusion.2), kind=kCustom, calls=%fused_computation | custom fusion | bytes 262656 | tf_op jit(solution)/shard_map/jit(_take)/gather | solution.py:73
  10.6 0.7 fusion.66
  11.2 1.3 collective-permute-start.3
  12.5 5.5 %collective-permute-start.2 = (bf16[32,512]{1,0:T(8,128)(2,1)}, bf16[32,512]{1,0:T(8,128)(2,1)S(1)}, u32[]{:S(2)}, u32[]{:S(2)}) collective-permute-start(bf16[32,512]{1,0:T(8,128)(2,1)} %get-tuple-element.20), channel_id=1, source_target_pairs={{0,8},{8,16},{16,24},{1,9},{9,17},{17,25},{2,10},{10,18},{18,26},{... | collective-permute-start | bytes 98312 | tf_op jit(solution)/shard_map/ppermute | solution.py:17
  18.0 3.1 %collective-permute-start.1 = (bf16[32,512]{1,0:T(8,128)(2,1)}, bf16[32,512]{1,0:T(8,128)(2,1)S(1)}, u32[]{:S(2)}, u32[]{:S(2)}) collective-permute-start(bf16[32,512]{1,0:T(8,128)(2,1)} %get-tuple-element.21), channel_id=1, source_target_pairs={{1,0},{2,1},{3,2},{4,3},{5,4},{6,5},{7,6},{0,7},{9,8},{10,9},{11,1... | collective-permute-start | bytes 98312 | tf_op jit(solution)/shard_map/ppermute | solution.py:18
  21.1 0.9 constant_dynamic-update-slice_fusion.4
  22.0 0.7 compare_select_fusion.1
  22.7 0.7 compare_select_fusion
  23.4 2.7 %constant_dynamic-update-slice_fusion.7 = bf16[1536,1536]{1,0:T(8,128)(2,1)} fusion(bf16[1536,512]{1,0:T(8,128)(2,1)} %param.15), kind=kLoop, calls=%fused_computation.96 | loop fusion | bytes 3145728
  26.1 4.8 %gather_fusion.2 = bf16[1536,512]{1,0:T(8,128)(2,1)S(1)} fusion(bf16[512,512]{1,0:T(8,128)(2,1)S(1)} %bitcast.22, s32[2048]{0:T(1024)S(1)} %pad_clamp_fusion), kind=kCustom, calls=%fused_computation.2 | custom fusion | bytes 3151872 | tf_op jit(solution)/shard_map/gather | solution.py:86
  31.0 5.4 %gather_fusion.1 = bf16[1536,512]{1,0:T(8,128)(2,1)} fusion(bf16[256,512]{1,0:T(8,128)(2,1)S(1)} %constant_dynamic-update-slice_fusion, s32[2048]{0:T(1024)S(1)} %pad_clamp_fusion.1), kind=kCustom, calls=%fused_computation.1 | custom fusion | bytes 3151872 | tf_op jit(solution)/shard_map/gather | solution.py:86
  36.5 2.8 %constant_dynamic-update-slice_fusion.6 = bf16[1536,1536]{1,0:T(8,128)(2,1)} fusion(bf16[1536,1536]{1,0:T(8,128)(2,1)} %constant_dynamic-update-slice_fusion.7, bf16[1536,512]{1,0:T(8,128)(2,1)} %gather_fusion.1), kind=kLoop, calls=%fused_computation.95 | loop fusion | bytes 3145728
  39.3 1.3 constant_dynamic-update-slice_fusion.5
  40.6 4.5 %fusion.69 = f32[1536,512]{1,0:T(8,128)S(1)} fusion(bf16[1536,1536]{1,0:T(8,128)(2,1)} %constant_dynamic-update-slice_fusion.5, bf16[1536,512]{1,0:T(8,128)(2,1)S(1)} %copy-done.8), kind=kOutput, calls=%fused_computation.122 | convolution fusion | flops 2415919104 | bytes 9437184 | tf_op jit(solution)/shard_map/dot_general | solution.py:87
  45.1 1.2 fusion.67
  46.3 0.5 copy-done.14
  46.8 0.4 multiply_reduce_fusion.1
  47.2 0.3 copy-done.6
  47.5 1.2 fusion.24
  48.7 0.7 fusion.32
  49.4 0.3 copy-done.9
  49.8 0.5 fusion.68
  50.3 0.5 copy-done.13
  50.8 0.4 copy-done.4
  51.1 0.4 fusion.27
  51.6 1.3 %fusion.63 = (f32[512]{0:T(512)S(1)}, f32[512,512]{1,0:T(8,128)S(1)}, bf16[512,512]{1,0:T(8,128)(2,1)}) fusion(f32[512]{0:T(512)S(1)} %get-tuple-element.23, f32[512,512]{1,0:T(8,128)S(1)} %get-tuple-element.28, f32[512]{0:T(512)S(1)} %broadcast_multiply_fusion.1, f32[512]{0:T(512)S(1)} %get-tuple-element.24, f32[512]{0:T(512)S(1)} %copy-done.5, ...), kind=kLoop, calls=%fused_computation.116 | loop fusion | flops 3407360 | bytes 3680256 | tf_op jit(solution)/shard_map/transpose(jvp())/reduce_sum | solution.py:29
  52.9 3.6 %convolution_convert_fusion.1 = bf16[512,1024]{1,0:T(8,128)(2,1)} fusion(bf16[1024,512]{1,0:T(8,128)(2,1)S(1)} %copy-done, f32[512,512]{1,0:T(8,128)} %copy-done.13, bf16[512,512]{1,0:T(8,128)(2,1)} %param.23, f32[512,512]{1,0:T(8,128)S(1)} %get-tuple-element.7, f32[512]{0:T(512)S(1)} %negate_multiply_fusion.1), kind=kOutput, calls=%fused_computation.40 | convolution fusion | flops 808976384 | bytes 4720640 | tf_op jit(solution)/shard_map/transpose(jvp())/dot_general | solution.py:44
  56.5 3.5 %multiply_reduce_fusion = (f32[1536]{0:T(1024)S(1)}, bf16[1536,512]{0,1:T(8,128)(2,1)S(1)}) fusion(f32[1536,512]{0,1:T(8,128)} %copy-done.2, f32[512]{0:T(512)S(1)} %copy-done.7, f32[1536]{0:T(1024)S(1)} %broadcast_multiply_fusion, bf16[512,1024]{1,0:T(8,128)(2,1)} %convolution_convert_fusion.1, s32[1536]{0:T(1024)S(1)} %copy-done.6), kind=kOutput, calls=%fused_computation.19 | convolution fusion | flops 810809856 | bytes 5263360 | tf_op jit(solution)/shard_map/transpose(jvp())/dot_general | solution.py:42
  60.0 0.9 fusion.45
  61.0 1.0 copy-done.15
  62.1 2.4 %fusion.1 = bf16[1536,512]{1,0:T(8,128)(2,1)S(1)} fusion(f32[1536,512]{1,0:T(8,128)S(1)} %copy-done.15, bf16[512,512]{1,0:T(8,128)(2,1)S(1)} %copy-done.11, f32[1536]{0:T(1024)S(1)} %negate_multiply_fusion, bf16[1536,512]{0,1:T(8,128)(2,1)S(1)} %get-tuple-element.30, f32[1536,512]{0,1:T(8,128)S(1)} %copy-done.3, f32[1536]{0:T(1024)S(1)} %multiply_multiply_fusion, ...), kind=kOutput, calls=%fused_computation.11 | convolution fusion | flops 821035008 | bytes 9988096 | tf_op jit(solution)/shard_map/transpose(jvp())/dot_general | solution.py:36
  64.5 1.2 copy-done.12
  65.7 3.8 %convolution_convert_fusion = bf16[1536,512]{1,0:T(8,128)(2,1)} fusion(bf16[1536,1536]{1,0:T(8,128)(2,1)S(1)} %bitcast.28, bf16[1536,512]{1,0:T(8,128)(2,1)S(1)} %fusion.1), kind=kOutput, calls=%fused_computation.30 | convolution fusion | flops 2416705536 | bytes 7864320 | tf_op jit(solution)/shard_map/dot_general | solution.py:134
  69.5 6.2 %fusion.36 = f32[1536,1024]{1,0:T(8,128)} fusion(bf16[1536,512]{1,0:T(8,128)(2,1)} %copy-done.12, bf16[1536,512]{1,0:T(8,128)(2,1)} %param.19), kind=kOutput, calls=%fused_computation.56 | convolution fusion | flops 1610612736 | bytes 8912896 | tf_op jit(solution)/shard_map/dot_general | solution.py:98
  75.6 10.6 %scatter_custom_fusion.1 = f32[256,512]{1,0:T(8,128)S(1)} fusion(s32[1536]{0:T(1024)} %param.16, f32[1536,1024]{1,0:T(8,128)} %fusion.36, f32[]{:T(128)} %constant.44.clone.1), kind=kCustom, calls=%fused_computation.13 | custom fusion | flops 786432 | bytes 3670528 | tf_op jit(solution)/shard_map/scatter-add | solution.py:104
  86.4 1.3 collective-permute-start.7
  87.7 4.9 %collective-permute-start.6 = (bf16[32,512]{1,0:T(8,128)(2,1)S(1)}, bf16[32,512]{1,0:T(8,128)(2,1)S(1)}, u32[]{:S(2)}, u32[]{:S(2)}) collective-permute-start(bf16[32,512]{1,0:T(8,128)(2,1)S(1)} %get-tuple-element.11), channel_id=1, source_target_pairs={{0,8},{8,16},{16,24},{1,9},{9,17},{17,25},{2,10},{10,18},{18,26},{... | collective-permute-start | bytes 98312 | tf_op jit(solution)/shard_map/ppermute | solution.py:17
  92.6 1.2 convert_add_fusion
  93.8 10.9 %scatter_custom_fusion = f32[512,512]{1,0:T(8,128)S(1)} fusion(f32[512,512]{1,0:T(8,128)S(1)} %convert_add_fusion, s32[1536]{0:T(1024)S(1)} %copy-done.6, f32[1536,1024]{1,0:T(8,128)} %fusion.36), kind=kCustom, calls=%fused_computation.15 | custom fusion | flops 786432 | bytes 4194304 | tf_op jit(solution)/shard_map/scatter-add | solution.py:107
  104.7 0.9 convert_element_type.93
  105.5 3.5 %collective-permute-start.5 = (bf16[32,512]{1,0:T(8,128)(2,1)S(1)}, bf16[32,512]{1,0:T(8,128)(2,1)S(1)}, u32[]{:S(2)}, u32[]{:S(2)}) collective-permute-start(bf16[32,512]{1,0:T(8,128)(2,1)S(1)} %get-tuple-element.12), channel_id=1, source_target_pairs={{1,0},{2,1},{3,2},{4,3},{5,4},{6,5},{7,6},{0,7},{9,8},{10,9},{11,1... | collective-permute-start | bytes 98312 | tf_op jit(solution)/shard_map/ppermute | solution.py:18
  109.1 1.6 %collective-permute-done.4 = bf16[32,512]{1,0:T(8,128)(2,1)S(1)} collective-permute-done((bf16[32,512]{1,0:T(8,128)(2,1)S(1)}, bf16[32,512]{1,0:T(8,128)(2,1)S(1)}, u32[]{:S(2)}, u32[]{:S(2)}) %collective-permute-start.4) | collective-permute-done | bytes 32800 | tf_op jit(solution)/shard_map/ppermute | solution.py:17
  110.7 1.6 %scatter_custom_fusion.2 = f32[128,512]{1,0:T(8,128)S(1)} fusion(f32[128,512]{1,0:T(8,128)S(1)} %slice.96, s32[128]{0:T(128)} %param.18, f32[32,512]{1,0:T(8,128)S(1)} %get-tuple-element.18, f32[]{:T(128)} %constant.50, f32[32,512]{1,0:T(8,128)S(1)} %get-tuple-element.17, f32[32,512]{1,0:T(8,128)S(1)} %get-tuple-element.16, f32[32,512]{1,0:T(8,128)S(1)} %get-tuple-element.15), kind=kCustom, calls=%fused_computation.69 | custom fusion | flops 262144 | bytes 524800 | tf_op jit(solution)/shard_map/scatter-add | solution.py:129
  112.3 0.7 convert_element_type.96
  113.0 13.8 %all-gather = bf16[768,512]{1,0:T(8,128)(2,1)S(1)} all-gather(bf16[192,512]{1,0:T(8,128)(2,1)} %reduce-scatter.2.cloned.1.call-done), channel_id=2, replica_groups=mesh['band'=4,'sector'=8] {'band'}, dimensions={0}, use_global_device_ids=true | all-gather | bytes 983040 | tf_op jit(solution)/shard_map/all_gather | solution.py:141
  126.9 0.8 convert_multiply_fusion.6
  (64 shorter events, 0.7 us)
Async XLA Ops:
  7.2 41.5 %copy-start = (bf16[1024,512]{1,0:T(8,128)(2,1)S(1)}, bf16[1024,512]{1,0:T(8,128)(2,1)}, u32[]{:S(2)}) copy-start(bf16[1024,512]{1,0:T(8,128)(2,1)} %param.22) | copy-start | bytes 3145732
  7.2 18.9 %copy-start.1 = (bf16[8,64,512]{2,1,0:T(8,128)(2,1)S(1)}, bf16[8,64,512]{2,1,0:T(8,128)(2,1)}, u32[]{:S(2)}) copy-start(bf16[8,64,512]{2,1,0:T(8,128)(2,1)} %param.13) | copy-start | bytes 1572868
  7.2 105.8 %reduce-scatter.2.cloned.1.call-start = ((), (), s32[]{:S(2)}) async-start(), calls=%async_computation.1 | async-start | bytes 1769472 | tf_op jit(solution)/shard_map/reduce_scatter | solution.py:133
  11.2 19.8 %collective-permute-start.3 = (bf16[32,512]{1,0:T(8,128)(2,1)}, bf16[32,512]{1,0:T(8,128)(2,1)S(1)}, u32[]{:S(2)}, u32[]{:S(2)}) collective-permute-start(bf16[32,512]{1,0:T(8,128)(2,1)} %get-tuple-element.19), channel_id=1, source_target_pairs={{8,0},{16,8},{24,16},{9,1},{17,9},{25,17},{10,2},{18,10},{26,18},{... | collective-permute-start | bytes 98312 | tf_op jit(solution)/shard_map/ppermute | solution.py:18
  12.5 18.5 %collective-permute-start.2 = (bf16[32,512]{1,0:T(8,128)(2,1)}, bf16[32,512]{1,0:T(8,128)(2,1)S(1)}, u32[]{:S(2)}, u32[]{:S(2)}) collective-permute-start(bf16[32,512]{1,0:T(8,128)(2,1)} %get-tuple-element.20), channel_id=1, source_target_pairs={{0,8},{8,16},{16,24},{1,9},{9,17},{17,25},{2,10},{10,18},{18,26},{... | collective-permute-start | bytes 98312 | tf_op jit(solution)/shard_map/ppermute | solution.py:17
  18.0 12.9 %collective-permute-start.1 = (bf16[32,512]{1,0:T(8,128)(2,1)}, bf16[32,512]{1,0:T(8,128)(2,1)S(1)}, u32[]{:S(2)}, u32[]{:S(2)}) collective-permute-start(bf16[32,512]{1,0:T(8,128)(2,1)} %get-tuple-element.21), channel_id=1, source_target_pairs={{1,0},{2,1},{3,2},{4,3},{5,4},{6,5},{7,6},{0,7},{9,8},{10,9},{11,1... | collective-permute-start | bytes 98312 | tf_op jit(solution)/shard_map/ppermute | solution.py:18
  21.1 9.9 %collective-permute-start = (bf16[32,512]{1,0:T(8,128)(2,1)}, bf16[32,512]{1,0:T(8,128)(2,1)S(1)}, u32[]{:S(2)}, u32[]{:S(2)}) collective-permute-start(bf16[32,512]{1,0:T(8,128)(2,1)} %get-tuple-element.22), channel_id=1, source_target_pairs={{0,1},{1,2},{2,3},{3,4},{4,5},{5,6},{6,7},{7,0},{8,9},{9,10},{10,1... | collective-permute-start | bytes 98312 | tf_op jit(solution)/shard_map/ppermute | solution.py:17
  36.5 4.1 %copy-start.8 = (bf16[1536,512]{1,0:T(8,128)(2,1)S(1)}, bf16[1536,512]{1,0:T(8,128)(2,1)}, u32[]{:S(2)}) copy-start(bf16[1536,512]{1,0:T(8,128)(2,1)} %param.19) | copy-start | bytes 4718596
  40.6 4.5 %copy-start.10 = (bf16[512,512]{1,0:T(8,128)(2,1)S(1)}, bf16[512,512]{1,0:T(8,128)(2,1)}, u32[]{:S(2)}) copy-start(bf16[512,512]{1,0:T(8,128)(2,1)} %param.20) | copy-start | bytes 1572868
  45.1 1.7 %copy-start.14 = (f32[1536,512]{1,0:T(8,128)}, f32[1536,512]{1,0:T(8,128)S(1)}, u32[]{:S(2)}) copy-start(f32[1536,512]{1,0:T(8,128)S(1)} %fusion.69) | copy-start | bytes 9437188
  46.8 1.9 %copy-start.2 = (f32[1536,512]{0,1:T(8,128)}, f32[1536,512]{0,1:T(8,128)S(1)}, u32[]{:S(2)}) copy-start(f32[1536,512]{0,1:T(8,128)S(1)} %get-tuple-element.26) | copy-start | bytes 9437188
  46.8 0.7 copy-start.6
  46.8 0.7 copy-start.7
  48.7 1.0 copy-start.9
  49.7 1.0 copy-start.13
  49.7 1.4 %copy-start.4 = (bf16[8,64,512]{2,1,0:T(8,128)(2,1)S(1)}, bf16[8,64,512]{2,1,0:T(8,128)(2,1)}, u32[]{:S(2)}) copy-start(bf16[8,64,512]{2,1,0:T(8,128)(2,1)} %param.25) | copy-start | bytes 1572868
  49.8 1.4 %copy-start.5 = (f32[512]{0:T(512)S(1)}, f32[512]{0:T(512)}, u32[]{:S(2)}) copy-start(f32[512]{0:T(512)} %param.24) | copy-start | bytes 6148
  56.5 3.5 %copy-start.3 = (f32[1536,512]{0,1:T(8,128)S(1)}, f32[1536,512]{0,1:T(8,128)}, u32[]{:S(2)}) copy-start(f32[1536,512]{0,1:T(8,128)} %copy-done.2) | copy-start | bytes 9437188
  60.0 1.0 copy-start.11
  60.0 2.1 %copy-start.15 = (f32[1536,512]{1,0:T(8,128)S(1)}, f32[1536,512]{1,0:T(8,128)}, u32[]{:S(2)}) copy-start(f32[1536,512]{1,0:T(8,128)} %copy-done.14) | copy-start | bytes 9437188
  60.0 5.7 %slice-start = ((s8[4718592]{0:T(1024)(128)(4,1)}), s8[4194304]{0:T(1024)(128)(4,1)S(1)}, s32[]{:S(2)}) async-start(s8[4718592]{0:T(1024)(128)(4,1)} %bitcast.27), calls=%async_computation.2 | async-start | bytes 8388608
  62.1 3.6 %slice-start.1 = ((s8[4718592]{0:T(1024)(128)(4,1)}), s8[524288]{0:T(1024)(128)(4,1)S(1)}, s32[]{:S(2)}) async-start(s8[4718592]{0:T(1024)(128)(4,1)} %bitcast.27), calls=%async_computation.3 | async-start | bytes 1048576
  64.5 1.2 copy-start.12
  86.4 22.7 %collective-permute-start.7 = (bf16[32,512]{1,0:T(8,128)(2,1)S(1)}, bf16[32,512]{1,0:T(8,128)(2,1)S(1)}, u32[]{:S(2)}, u32[]{:S(2)}) collective-permute-start(bf16[32,512]{1,0:T(8,128)(2,1)S(1)} %get-tuple-element.10), channel_id=1, source_target_pairs={{8,0},{16,8},{24,16},{9,1},{17,9},{25,17},{10,2},{18,10},{26,18},{... | collective-permute-start | bytes 98312 | tf_op jit(solution)/shard_map/ppermute | solution.py:18
  87.7 21.4 %collective-permute-start.6 = (bf16[32,512]{1,0:T(8,128)(2,1)S(1)}, bf16[32,512]{1,0:T(8,128)(2,1)S(1)}, u32[]{:S(2)}, u32[]{:S(2)}) collective-permute-start(bf16[32,512]{1,0:T(8,128)(2,1)S(1)} %get-tuple-element.11), channel_id=1, source_target_pairs={{0,8},{8,16},{16,24},{1,9},{9,17},{17,25},{2,10},{10,18},{18,26},{... | collective-permute-start | bytes 98312 | tf_op jit(solution)/shard_map/ppermute | solution.py:17
  105.5 5.1 %collective-permute-start.4 = (bf16[32,512]{1,0:T(8,128)(2,1)S(1)}, bf16[32,512]{1,0:T(8,128)(2,1)S(1)}, u32[]{:S(2)}, u32[]{:S(2)}) collective-permute-start(bf16[32,512]{1,0:T(8,128)(2,1)S(1)} %get-tuple-element.9), channel_id=1, source_target_pairs={{0,1},{1,2},{2,3},{3,4},{4,5},{5,6},{6,7},{7,0},{8,9},{9,10},{10,1... | collective-permute-start | bytes 98312 | tf_op jit(solution)/shard_map/ppermute | solution.py:17
  105.5 5.1 %collective-permute-start.5 = (bf16[32,512]{1,0:T(8,128)(2,1)S(1)}, bf16[32,512]{1,0:T(8,128)(2,1)S(1)}, u32[]{:S(2)}, u32[]{:S(2)}) collective-permute-start(bf16[32,512]{1,0:T(8,128)(2,1)S(1)} %get-tuple-element.12), channel_id=1, source_target_pairs={{1,0},{2,1},{3,2},{4,3},{5,4},{6,5},{7,6},{0,7},{9,8},{10,9},{11,1... | collective-permute-start | bytes 98312 | tf_op jit(solution)/shard_map/ppermute | solution.py:18
Sparse Core Ops, SparseCore 0:
  69.6 35.3 reduce-scatter.1
